TPU v7x, 256 devices: a whole 4x4x8 slice. The times are simulated.
256 devices in a mesh: buf: 32 (over x, y, core), lat: 8 (over z).
Axes of the slice: x: 4, y: 4, z: 8, core: 2. Of those that a mesh axis runs over, the one named last changes fastest.
Arguments:
- buffer: bfloat16 [8192, 4096], P('buf'), may hold values from -6 to 6
- sample_rows: int32 [8192], P('lat'), may hold values from 0 to 8191, as said below
- window: bfloat16 [24576, 4096], P('buf'), may hold values from -6 to 6
- enc_scale: float32 [8192], P('lat'), may hold values from 0.5 to 2
- dec_bias: float32 [4096], replicated, may hold values from -3 to 3
Outputs:
- recon: bfloat16 [24576, 4096], P('buf', 'lat')
Inputs may be any that keep to these rules, and one draw needn't show every extreme that they name: `sample_rows`: entry k names the buffer row sampled for reseeded latent k; shard s of the buffer holds rows s * 256 to (s + 1) * 256 - 1. In each aligned block of 32 entries at most 2 name rows of one shard, and in every block some shard gives exactly 2. In each owner's 1024 entries at most 64 name rows of one shard, and some shard gives exactly 64.
All inputs are finite; a program needn't handle non-finite values.
Results may differ from a plain program's by a relative error of at most 0.018.
Values may be sent and summed in bfloat16 or wider, within the bound.
A program may use at most 128 MiB of HBM per device.

v0:
```python
import jax
import jax.numpy as jnp
from jax import lax
from jax.sharding import PartitionSpec as P


def unit_rows(picked_rows):
    values = picked_rows.astype(jnp.float32)
    squares = jnp.sum(values * values, axis=1, keepdims=True)
    return (values * lax.rsqrt(squares + 1e-06)).astype(jnp.bfloat16)


def encode_block(centered, unit_block, scale_block):
    scores = lax.dot_general(
        centered, unit_block, (((1,), (1,)), ((), ())), preferred_element_type=jnp.float32
    )
    return jnp.maximum(scores * scale_block[None, :], 0.0).astype(jnp.bfloat16)


def pick_units(buffer, pick_index):
    picked = jnp.take(buffer, jnp.maximum(pick_index, 0), axis=0)
    picked = jnp.where((pick_index >= 0)[:, None], picked, jnp.zeros_like(picked))
    return unit_rows(picked)


def on_device(buffer, sample_rows, window, enc_scale, dec_bias):
    shard_count = lax.axis_size("buf")
    shard_index = lax.axis_index("buf")
    owner_count = sample_rows.shape[0]
    slot_count = owner_count // shard_count
    shard_rows = buffer.shape[0]
    capacity = 2 + (slot_count - 1) // shard_count
    source = sample_rows // shard_rows
    offset = sample_rows - source * shard_rows
    centered = (window.astype(jnp.float32) - dec_bias[None, :]).astype(jnp.bfloat16)
    positions = jnp.arange(owner_count, dtype=jnp.int32)
    own_capacity = shard_count * capacity
    matching = source[:, None] == source[None, :]
    earlier = positions[:, None] < positions[None, :]
    owner_rank = jnp.sum((matching & earlier).astype(jnp.int32), axis=0)
    room_iota = jnp.arange(own_capacity, dtype=jnp.int32)
    chosen = (source == shard_index)[:, None] & (owner_rank[:, None] == room_iota[None, :])
    pick_index = jnp.sum(jnp.where(chosen, offset[:, None] + 1, 0), axis=0) - 1
    packed = pick_units(buffer, pick_index)
    collected = lax.all_gather(packed, "buf", axis=0, tiled=True)
    all_units = jnp.take(collected, source * own_capacity + owner_rank, axis=0)
    active_all = encode_block(centered, all_units, enc_scale)
    partial_value = jnp.dot(active_all, all_units, preferred_element_type=jnp.float32)
    rounded = partial_value.astype(jnp.bfloat16).astype(jnp.float32)
    summed = lax.psum_scatter(
        rounded.astype(jnp.bfloat16), "lat", scatter_dimension=1, tiled=True
    ).astype(jnp.float32)
    feature_count = summed.shape[1]
    bias_part = lax.dynamic_slice_in_dim(
        dec_bias, lax.axis_index("lat") * feature_count, feature_count
    )
    return (summed + bias_part[None, :]).astype(jnp.bfloat16)


def solution(mesh):
    in_specs = (P("buf", None), P("lat"), P("buf", None), P("lat"), P())
    out_specs = P("buf", "lat")
    return jax.shard_map(
        on_device, mesh=mesh, in_specs=in_specs, out_specs=out_specs, check_vma=False
    )
```

profile of v0, /device:TPU:1, one launch (start us, length us, event | category | flops | bytes accessed | tf_op | source)
XLA Modules:
  0.0 220.5 jit_solution(11854953599494018754)
XLA Ops:
  6.5 0.0 copy-start
  6.5 0.0 all-gather.2.cloned.1.call-start
  6.5 0.8 add_select_fusion
  7.4 0.4 convert_reduce_fusion
  7.8 0.7 broadcast_clamp_fusion
  8.5 0.7 compare_and_fusion
  9.2 0.2 select_reduce_fusion
  9.4 0.0 copy-done
  9.4 0.9 gather_fusion
  10.3 0.3 fusion.3
  10.6 1.0 fusion.4
  11.7 0.0 all-gather.2.cloned.1.call-update
  11.7 0.0 reduce-scatter.2.cloned.1.call-start
  11.7 81.8 %all-gather.2.cloned.1.call-done = bf16[2048,4096]{1,0:T(8,128)(2,1)} async-done(((bf16[64,4096]{1,0:T(8,128)(2,1)}), bf16[2048,4096]{1,0:T(8,128)(2,1)}) %all-gather.2.cloned.1.call-update) | async-done | bytes 16777232 | tf_op jit(solution)/shard_map/all_gather | solution.py:45
  93.6 0.0 copy-start.2
  93.6 0.0 copy-start.3
  93.6 23.0 %gather_fusion.1 = bf16[1024,4096]{1,0:T(8,128)(2,1)} fusion(bf16[2048,4096]{1,0:T(8,128)(2,1)} %all-gather.2.cloned.1.call-done, s32[1024]{0:T(1024)S(1)} %get-tuple-element.7), kind=kCustom, calls=%fused_computation.1 | custom fusion | bytes 16781312 | tf_op jit(solution)/shard_map/jit(_take)/gather | solution.py:46
  116.6 0.0 copy-done.2
  116.6 0.0 copy-done.3
  116.6 0.0 copy-start.1
  116.6 11.6 %maximum_convert_fusion = bf16[768,1024]{1,0:T(8,128)(2,1)S(1)} fusion(bf16[1024,4096]{1,0:T(8,128)(2,1)} %gather_fusion.1, pred[1024]{0:T(1024)(128)(4,1)S(1)} %get-tuple-element.5, bf16[768,4096]{1,0:T(8,128)(2,1)} %param.7, f32[4096]{0:T(1024)S(1)} %copy-done.2, f32[1024]{0:T(1024)S(1)} %copy-done.3), kind=kOutput, calls=%fused_computation.10 | convolution fusion | flops 6458441728 | bytes 16274432 | tf_op jit(solution)/shard_map/dot_general | solution.py:14
  128.3 0.0 copy-done.1
  128.3 8.8 %convolution_convert_fusion = bf16[768,4096]{1,0:T(8,128)(2,1)} fusion(bf16[768,1024]{1,0:T(8,128)(2,1)S(1)} %maximum_convert_fusion, bf16[1024,4096]{1,0:T(8,128)(2,1)S(1)} %copy-done.1, pred[1024]{0:T(1024)(128)(4,1)S(1)} %get-tuple-element.5), kind=kOutput, calls=%fused_computation.4 | convolution fusion | flops 6449790976 | bytes 16253952 | tf_op jit(solution)/shard_map/dot_general | solution.py:48
  137.1 0.0 reduce-scatter.2.cloned.1.call-update
  137.1 0.1 dynamic_slice.3
  137.2 74.4 %reduce-scatter.2.cloned.1.call-done = bf16[768,512]{1,0:T(8,128)(2,1)} async-done(((bf16[768,4096]{1,0:T(8,128)(2,1)}), bf16[768,512]{1,0:T(8,128)(2,1)}) %reduce-scatter.2.cloned.1.call-update) | async-done | bytes 786448 | tf_op jit(solution)/shard_map/reduce_scatter | solution.py:50
  211.5 2.2 add_convert_fusion
  (4 shorter events, 0.0 us)
Async XLA Ops:
  6.5 2.9 %copy-start = (bf16[256,4096]{1,0:T(8,128)(2,1)S(1)}, bf16[256,4096]{1,0:T(8,128)(2,1)}, u32[]{:S(2)}) copy-start(bf16[256,4096]{1,0:T(8,128)(2,1)} %param.5) | copy-start | bytes 6291460
  6.5 87.0 %all-gather.2.cloned.1.call-start = ((), (), s32[]{:S(2)}) async-start(), calls=%async_computation.1 | async-start | bytes 17301504 | tf_op jit(solution)/shard_map/all_gather | solution.py:45
  11.7 199.9 %reduce-scatter.2.cloned.1.call-start = ((), (), s32[]{:S(2)}) async-start(), calls=%async_computation.2 | async-start | bytes 7077888 | tf_op jit(solution)/shard_map/reduce_scatter | solution.py:50
  93.6 23.0 %copy-start.2 = (f32[4096]{0:T(1024)S(1)}, f32[4096]{0:T(1024)}, u32[]{:S(2)}) copy-start(f32[4096]{0:T(1024)} %param.9) | copy-start | bytes 49156
  93.6 23.0 %copy-start.3 = (f32[1024]{0:T(1024)S(1)}, f32[1024]{0:T(1024)}, u32[]{:S(2)}) copy-start(f32[1024]{0:T(1024)} %param.8) | copy-start | bytes 12292
  116.6 11.7 %copy-start.1 = (bf16[1024,4096]{1,0:T(8,128)(2,1)S(1)}, bf16[1024,4096]{1,0:T(8,128)(2,1)}, u32[]{:S(2)}) copy-start(bf16[1024,4096]{1,0:T(8,128)(2,1)} %gather_fusion.1) | copy-start | bytes 25165828
Sparse Core Ops, SparseCore 0:
  11.8 81.7 all-gather.1
  137.2 74.2 reduce-scatter.1
where the time goes:
time: 221 us
  waiting for transfers between devices  156 us (71%)
  local copies, waits for them, and re-layouts  24 us (11%)
  matrix products  20.4 us (9%)
  between operations  13.5 us (6%)
  other arithmetic  6.37 us (3%)
    all_gather x1, waiting for transfers between devices, on_device(): collected = lax.all_gather(packed, 'buf', axis=0, tiled=True)  81.8 us
    reduce_scatter x1, waiting for transfers between devices, on_device(): lax.psum_scatter(rounded.astype(jnp.bfloat16), 'lat', scatter_dimension=1...  74.4 us
    gather x1, local copies, waits for them, and re-layouts, on_device(): all_units = jnp.take(collected, source * own_capacity + owner_rank, axis=0)  23 us
    dot_general x1, matrix products, encode_block(): lax.dot_general(centered, unit_block, (((1,), (1,)), ((), ())), preferred...  11.6 us
    dot_general x1, matrix products, on_device(): jnp.dot(active_all, all_units, preferred_element_type=jnp.float32)  8.79 us
  transfers between devices with their start and end apart: 2, of which 2 were waited for; matrix products, arithmetic and copies ran while one was open for 0% of the time, Pallas kernels for 0%

commit v1 on v0

--- a/solution.py
+++ b/solution.py
@@ -42,7 +42,13 @@
     chosen = (source == shard_index)[:, None] & (owner_rank[:, None] == room_iota[None, :])
     pick_index = jnp.sum(jnp.where(chosen, offset[:, None] + 1, 0), axis=0) - 1
     packed = pick_units(buffer, pick_index)
-    collected = lax.all_gather(packed, "buf", axis=0, tiled=True)
+    found = []
+    for _ in range(lax.psum(1, axis_name="buf")):
+        found.append(packed)
+    collected = jnp.concatenate(
+        lax.all_to_all(jnp.stack(found, axis=0), concat_axis=0, split_axis=0, axis_name="buf"),
+        axis=0,
+    )
     all_units = jnp.take(collected, source * own_capacity + owner_rank, axis=0)
     active_all = encode_block(centered, all_units, enc_scale)
     partial_value = jnp.dot(active_all, all_units, preferred_element_type=jnp.float32)

time: 221 us -> 334 us (1.51)
  blocking collectives: 0 us -> 194 us
  waiting for transfers between devices: 156 us -> 74.4 us
    all_to_all x0 -> x1, blocking collectives: none -> 194 us  [on_device(): lax.all_to_all(jnp.stack(found, axis=0), concat_axis=0, split_axis=0, axi...]
    all_gather x1 -> x0, waiting for transfers between devices: 81.8 us -> none  [on_device(): collected = lax.all_gather(packed, 'buf', axis=0, tiled=True)]
  transfers between devices with their start and end apart: 2 -> 1, of which waited for: 2 -> 1; matrix products, arithmetic and copies ran while one was open for 0% -> 0% of each run, Pallas kernels for 0% -> 0%
where the time goes in v1:
time: 334 us
  blocking collectives  194 us (58%)
  waiting for transfers between devices  74.4 us (22%)
  local copies, waits for them, and re-layouts  25.9 us (8%)
  matrix products  20.4 us (6%)
  between operations  13.5 us (4%)
  other arithmetic  5.58 us (2%)
    all_to_all x1, blocking collectives, on_device(): lax.all_to_all(jnp.stack(found, axis=0), concat_axis=0, split_axis=0, axi...  194 us
    reduce_scatter x1, waiting for transfers between devices, on_device(): lax.psum_scatter(rounded.astype(jnp.bfloat16), 'lat', scatter_dimension=1...  74.4 us
    gather x1, local copies, waits for them, and re-layouts, on_device(): all_units = jnp.take(collected, source * own_capacity + owner_rank, axis=0)  23 us
    dot_general x1, matrix products, encode_block(): lax.dot_general(centered, unit_block, (((1,), (1,)), ((), ())), preferred...  11.7 us
    dot_general x1, matrix products, on_device(): jnp.dot(active_all, all_units, preferred_element_type=jnp.float32)  8.79 us
  transfers between devices with their start and end apart: 1, of which 1 were waited for; matrix products, arithmetic and copies ran while one was open for 0% of the time, Pallas kernels for 0%

profile of v1, /device:TPU:1, one launch (start us, length us, event | category | flops | bytes accessed | tf_op | source)
XLA Modules:
  0.0 333.8 jit_solution(16674362965533190082)
XLA Ops:
  6.5 0.0 copy-start
  6.5 0.0 reduce-scatter.2.cloned.1.call-start
  6.5 0.8 add_select_fusion
  7.4 0.4 convert_reduce_fusion
  7.8 0.7 broadcast_clamp_fusion
  8.5 0.7 compare_and_fusion
  9.2 0.2 select_reduce_fusion
  9.4 0.0 copy-done
  9.4 0.9 gather_fusion
  10.3 0.4 fusion.3
  10.6 0.2 fusion.4
  10.9 2.0 stack.2
  12.9 193.9 %all_to_all.5 = bf16[32,64,4096]{2,1,0:T(8,128)(2,1)} all-to-all(bf16[32,64,4096]{2,1,0:T(8,128)(2,1)S(1)} %stack.2), channel_id=1, replica_groups=mesh['buf'=32,'lat'=8] {'buf'}, dimensions={0} | all-to-all | bytes 33554432 | tf_op jit(solution)/shard_map/all_to_all | solution.py:49
  206.8 0.0 copy-start.2
  206.8 0.0 copy-start.3
  206.8 23.0 %gather_fusion.1 = bf16[1024,4096]{1,0:T(8,128)(2,1)} fusion(bf16[2048,4096]{1,0:T(8,128)(2,1)} %bitcast.2, s32[1024]{0:T(1024)S(1)} %get-tuple-element.7), kind=kCustom, calls=%fused_computation.1 | custom fusion | bytes 16781312 | tf_op jit(solution)/shard_map/jit(_take)/gather | solution.py:52
  229.8 0.0 copy-done.2
  229.8 0.0 copy-done.3
  229.8 0.0 copy-start.1
  229.8 11.7 %maximum_convert_fusion = bf16[768,1024]{1,0:T(8,128)(2,1)S(1)} fusion(bf16[1024,4096]{1,0:T(8,128)(2,1)} %gather_fusion.1, pred[1024]{0:T(1024)(128)(4,1)S(1)} %get-tuple-element.5, bf16[768,4096]{1,0:T(8,128)(2,1)} %param.7, f32[4096]{0:T(1024)S(1)} %copy-done.2, f32[1024]{0:T(1024)S(1)} %copy-done.3), kind=kOutput, calls=%fused_computation.10 | convolution fusion | flops 6458441728 | bytes 16274432 | tf_op jit(solution)/shard_map/dot_general | solution.py:14
  241.5 0.0 copy-done.1
  241.5 8.8 %convolution_convert_fusion = bf16[768,4096]{1,0:T(8,128)(2,1)} fusion(bf16[768,1024]{1,0:T(8,128)(2,1)S(1)} %maximum_convert_fusion, bf16[1024,4096]{1,0:T(8,128)(2,1)S(1)} %copy-done.1, pred[1024]{0:T(1024)(128)(4,1)S(1)} %get-tuple-element.5), kind=kOutput, calls=%fused_computation.4 | convolution fusion | flops 6449790976 | bytes 16253952 | tf_op jit(solution)/shard_map/dot_general | solution.py:54
  250.3 0.0 reduce-scatter.2.cloned.1.call-update
  250.3 0.1 dynamic_slice.3
  250.4 74.4 %reduce-scatter.2.cloned.1.call-done = bf16[768,512]{1,0:T(8,128)(2,1)} async-done(((bf16[768,4096]{1,0:T(8,128)(2,1)}), bf16[768,512]{1,0:T(8,128)(2,1)}) %reduce-scatter.2.cloned.1.call-update) | async-done | bytes 786448 | tf_op jit(solution)/shard_map/reduce_scatter | solution.py:56
  324.8 2.2 add_convert_fusion
  (4 shorter events, 0.0 us)
Async XLA Ops:
  6.5 2.9 copy-start
  6.5 318.2 %reduce-scatter.2.cloned.1.call-start = ((), (), s32[]{:S(2)}) async-start(), calls=%async_computation.2 | async-start | bytes 7077888 | tf_op jit(solution)/shard_map/reduce_scatter | solution.py:56
  206.8 23.0 %copy-start.2 = (f32[4096]{0:T(1024)S(1)}, f32[4096]{0:T(1024)}, u32[]{:S(2)}) copy-start(f32[4096]{0:T(1024)} %param.9) | copy-start | bytes 49156
  206.8 23.0 %copy-start.3 = (f32[1024]{0:T(1024)S(1)}, f32[1024]{0:T(1024)}, u32[]{:S(2)}) copy-start(f32[1024]{0:T(1024)} %param.8) | copy-start | bytes 12292
  229.8 11.7 %copy-start.1 = (bf16[1024,4096]{1,0:T(8,128)(2,1)S(1)}, bf16[1024,4096]{1,0:T(8,128)(2,1)}, u32[]{:S(2)}) copy-start(bf16[1024,4096]{1,0:T(8,128)(2,1)} %gather_fusion.1) | copy-start | bytes 25165828
Sparse Core Ops, SparseCore 0:
  250.4 74.2 reduce-scatter.1
